TPU v7x, 768 devices: a whole 4x8x12 slice. The times are simulated.
768 devices in a mesh: ctx: 192 (over x, y, z_hi, core), tp: 4 (over z_lo).
Axes of the slice: x: 4, y: 8, z: 12 (z_hi: 3, z_lo: 4; z = z_hi * 4 + z_lo), core: 2. Of those that a mesh axis runs over, the one named last changes fastest.
Arguments:
- queries: bfloat16 [49152, 2048], P('ctx', 'tp'), may hold values from -70 to 70
- keys: bfloat16 [49152, 1024], P('ctx', 'tp'), may hold values from -6 to 6
- values: bfloat16 [49152, 1024], P('ctx', 'tp'), may hold values from -6 to 6
- grad_out: bfloat16 [49152, 5376], P(('ctx', 'tp')), may hold values from -24 to 24
- out_weight: bfloat16 [2048, 5376], P('tp'), may hold values from -0.078125 to 0.078125
Outputs:
- grad_queries: float32 [49152, 2048], P('ctx', 'tp')
- grad_keys: float32 [49152, 1024], P('ctx', 'tp')
- grad_values: float32 [49152, 1024], P('ctx', 'tp')
All inputs are finite; a program needn't handle non-finite values.
Results may differ from a plain program's by a relative error of at most 0.014.
Values may be sent and summed in bfloat16 or wider, within the bound.
A program may use at most 64 MiB of HBM per device.

v0:
```python
import jax
import jax.numpy as jnp
from jax import lax
from jax.sharding import PartitionSpec as P

HD = 128
WIN = 1024


score_scale = 168.0 ** (-0.5)


def passed_along(block, axis, distance):
    devices = range(lax.axis_size(axis))
    route = [(i - distance, i) for i in devices if i - distance in devices]
    return lax.ppermute(block, axis, route)


def band_grads(queries, dout, key_span, value_span, query_pos, key_pos, kv_heads):
    shard_rows = queries.shape[0]
    span_rows = key_span.shape[0]
    group_size = queries.shape[1] // (kv_heads * HD)
    query_heads = queries.reshape(shard_rows, kv_heads, group_size, HD)
    dout_heads = dout.reshape(shard_rows, kv_heads, group_size, HD)
    key_heads = key_span.reshape(span_rows, kv_heads, HD)
    value_heads = value_span.reshape(span_rows, kv_heads, HD)
    scores = (
        jnp.einsum("sgrd,egd->grse", query_heads, key_heads, preferred_element_type=jnp.float32)
        * score_scale
    )
    allowed = (
        (key_pos[None, :] <= query_pos[:, None])
        & (key_pos[None, :] > query_pos[:, None] - WIN)
        & (key_pos[None, :] >= 0)
    )
    scores = jnp.where(allowed, scores, -1e30)
    row_max = jnp.max(scores, axis=-1, keepdims=True)
    weights = jnp.where(allowed, jnp.exp(scores - row_max), 0.0)
    probability = weights / jnp.sum(weights, axis=-1, keepdims=True)
    dprobs = jnp.einsum(
        "sgrd,egd->grse", dout_heads, value_heads, preferred_element_type=jnp.float32
    )
    row_delta = jnp.sum(probability * dprobs, axis=-1, keepdims=True)
    dscores = probability * (dprobs - row_delta)
    probs_low = probability.astype(jnp.bfloat16)
    dscores_low = dscores.astype(jnp.bfloat16)
    grad_value = jnp.einsum(
        "grse,sgrd->egd", probs_low, dout_heads, preferred_element_type=jnp.float32
    )
    grad_query = score_scale * jnp.einsum(
        "grse,egd->sgrd", dscores_low, key_heads, preferred_element_type=jnp.float32
    )
    grad_key = score_scale * jnp.einsum(
        "grse,sgrd->egd", dscores_low, query_heads, preferred_element_type=jnp.float32
    )
    return (
        grad_query.reshape(shard_rows, -1),
        grad_key.reshape(span_rows, -1),
        grad_value.reshape(span_rows, -1),
    )


def on_device(queries, keys, values, grad_out, out_weight):
    shard_rows = queries.shape[0]
    kv_width = keys.shape[1]
    kv_heads = kv_width // HD
    blocks = WIN // shard_rows
    product = lax.dot_general(
        lax.all_gather(grad_out, "tp", axis=0, tiled=True),
        out_weight,
        (((1,), (1,)), ((), ())),
        preferred_element_type=jnp.float32,
    )
    dout = product.astype(jnp.bfloat16)
    key_value = jnp.stack([keys, values])
    shifted = []
    for distance in range(blocks, 0, -1):
        shifted.append(passed_along(key_value, "ctx", distance))
    extended = jnp.concatenate(shifted + [key_value], axis=1)
    shard = lax.axis_index("ctx")
    span_rows = extended.shape[1]
    query_pos = shard * shard_rows + jnp.arange(shard_rows, dtype=jnp.int32)
    key_pos = shard * shard_rows - blocks * shard_rows + jnp.arange(span_rows, dtype=jnp.int32)
    grad_query, grad_key, grad_value = band_grads(
        queries, dout, extended[0], extended[1], query_pos, key_pos, kv_heads
    )
    span_grads = jnp.stack([grad_key, grad_value])
    earlier_low = span_grads[:, : blocks * shard_rows].astype(jnp.bfloat16)
    summed = span_grads[:, blocks * shard_rows :]
    for offset in range(blocks):
        distance = blocks - offset
        block_grads = earlier_low[:, offset * shard_rows : (offset + 1) * shard_rows]
        returned = passed_along(block_grads, "ctx", -distance)
        summed = summed + returned.astype(jnp.float32)
    return (grad_query, summed[0], summed[1])


def solution(mesh):
    in_specs = (
        P("ctx", "tp"),
        P("ctx", "tp"),
        P("ctx", "tp"),
        P(("ctx", "tp"), None),
        P("tp", None),
    )
    out_specs = (P("ctx", "tp"), P("ctx", "tp"), P("ctx", "tp"))
    return jax.shard_map(
        on_device, mesh=mesh, in_specs=in_specs, out_specs=out_specs, check_vma=False
    )
```

profile of v0, /device:TPU:56, one launch (start us, length us, event | category | flops | bytes accessed | tf_op | source)
XLA Modules:
  0.0 213.1 jit_solution(10591616458433517837)
XLA Ops:
  7.2 0.0 all-gather.2.cloned.1.call-start
  7.2 0.7 all-gather.2.cloned.1.call-update
  7.9 1.0 copy.19
  8.9 1.0 copy.20
  10.0 14.6 %collective-permute-start = (bf16[2,256,256]{1,2,0:T(8,128)(2,1)S(1)}, bf16[2,256,256]{1,2,0:T(8,128)(2,1)S(1)}, u32[]{:S(2)}, u32[]{:S(2)}) collective-permute-start(bf16[2,256,256]{1,2,0:T(8,128)(2,1)S(1)} %pad_maximum_fusion.1), channel_id=1, source_target_pairs={{0,16},{4,20},{8,24},{12,28},{16,32},{20,36},{24,40},{28,44},{32,4... | collective-permute-start | bytes 786440 | tf_op jit(solution)/shard_map/ppermute | solution.py:16
  24.5 1.9 collective-permute-start.1
  26.4 4.3 %collective-permute-start.2 = (bf16[2,256,256]{1,2,0:T(8,128)(2,1)S(1)}, bf16[2,256,256]{1,2,0:T(8,128)(2,1)S(1)}, u32[]{:S(2)}, u32[]{:S(2)}) collective-permute-start(bf16[2,256,256]{1,2,0:T(8,128)(2,1)S(1)} %pad_maximum_fusion.1), channel_id=1, source_target_pairs={{0,8},{4,12},{8,16},{12,20},{16,24},{20,28},{24,32},{28,36},{32,40... | collective-permute-start | bytes 786440 | tf_op jit(solution)/shard_map/ppermute | solution.py:16
  30.8 5.4 %collective-permute-start.3 = (bf16[2,256,256]{1,2,0:T(8,128)(2,1)S(1)}, bf16[2,256,256]{1,2,0:T(8,128)(2,1)S(1)}, u32[]{:S(2)}, u32[]{:S(2)}) collective-permute-start(bf16[2,256,256]{1,2,0:T(8,128)(2,1)S(1)} %pad_maximum_fusion.1), channel_id=1, source_target_pairs={{0,4},{4,8},{8,12},{12,16},{16,20},{20,24},{24,28},{28,32},{32,36}... | collective-permute-start | bytes 786440 | tf_op jit(solution)/shard_map/ppermute | solution.py:16
  36.2 1.0 and_and_fusion
  37.2 0.0 copy-start
  37.2 1.2 copy.45
  38.4 8.0 %collective-permute-done = bf16[2,256,256]{1,2,0:T(8,128)(2,1)S(1)} collective-permute-done((bf16[2,256,256]{1,2,0:T(8,128)(2,1)S(1)}, bf16[2,256,256]{1,2,0:T(8,128)(2,1)S(1)}, u32[]{:S(2)}, u32[]{:S(2)}) %collective-permute-start) | collective-permute-done | bytes 262176 | tf_op jit(solution)/shard_map/ppermute | solution.py:16
  46.5 2.2 %collective-permute-done.1 = bf16[2,256,256]{1,2,0:T(8,128)(2,1)S(1)} collective-permute-done((bf16[2,256,256]{1,2,0:T(8,128)(2,1)S(1)}, bf16[2,256,256]{1,2,0:T(8,128)(2,1)S(1)}, u32[]{:S(2)}, u32[]{:S(2)}) %collective-permute-start.1) | collective-permute-done | bytes 262176 | tf_op jit(solution)/shard_map/ppermute | solution.py:16
  48.7 20.1 %collective-permute-done.2 = bf16[2,256,256]{1,2,0:T(8,128)(2,1)S(1)} collective-permute-done((bf16[2,256,256]{1,2,0:T(8,128)(2,1)S(1)}, bf16[2,256,256]{1,2,0:T(8,128)(2,1)S(1)}, u32[]{:S(2)}, u32[]{:S(2)}) %collective-permute-start.2) | collective-permute-done | bytes 262176 | tf_op jit(solution)/shard_map/ppermute | solution.py:16
  68.8 8.1 %collective-permute-done.3 = bf16[2,256,256]{1,2,0:T(8,128)(2,1)S(1)} collective-permute-done((bf16[2,256,256]{1,2,0:T(8,128)(2,1)S(1)}, bf16[2,256,256]{1,2,0:T(8,128)(2,1)S(1)}, u32[]{:S(2)}, u32[]{:S(2)}) %collective-permute-start.3) | collective-permute-done | bytes 262176 | tf_op jit(solution)/shard_map/ppermute | solution.py:16
  77.0 0.1 fusion.21
  77.1 4.8 %fusion.6 = (f32[2,2,256]{2,1,0:T(2,128)S(1)}, f32[2,2,256,1280]{2,3,1,0:T(8,128)}) fusion(pred[256,1280]{0,1:T(8,128)(4,1)S(1)} %and_and_fusion, bf16[1280,2,128,1]{0,2,3,1:T(8,128)(2,1)S(1)} %bitcast.75, bf16[256,2,2,128]{0,3,2,1:T(8,128)(2,1)S(1)} %bitcast.84), kind=kOutput, calls=%fused_computation.10 | convolution fusion | flops 342099200 | bytes 6492160 | tf_op jit(solution)/shard_map/sub | solution.py:38
  81.9 38.4 %all-gather.2.cloned.1.call-done = bf16[256,5376]{1,0:T(8,128)(2,1)} async-done(((bf16[64,5376]{1,0:T(8,128)(2,1)}), bf16[256,5376]{1,0:T(8,128)(2,1)}) %all-gather.2.cloned.1.call-update) | async-done | bytes 2752528 | tf_op jit(solution)/shard_map/all_gather | solution.py:69
  120.3 5.0 %convolution_convert_fusion = bf16[256,512]{1,0:T(8,128)(2,1)S(1)} fusion(bf16[256,5376]{1,0:T(8,128)(2,1)} %all-gather.2.cloned.1.call-done, bf16[512,5376]{1,0:T(8,128)(2,1)} %param.9), kind=kOutput, calls=%fused_computation.21 | convolution fusion | flops 1409417216 | bytes 8519680 | tf_op jit(solution)/shard_map/dot_general | solution.py:68
  125.3 0.1 copy.46
  125.5 4.1 %fusion.9 = f32[2,128,1280,1]{2,1,3,0:T(8,128)} fusion(bf16[256,2,2,128]{0,3,2,1:T(8,128)(2,1)S(1)} %bitcast.88, f32[2,2,256]{2,1,0:T(2,128)S(1)} %get-tuple-element.17, pred[256,1280]{0,1:T(8,128)(4,1)S(1)} %and_and_fusion, bf16[1280,2,128,1]{0,2,3,1:T(8,128)(2,1)S(1)} %bitcast.76, bf16[256,2,2,128]{0,3,2,1:T(8,128)(2,1)S(1)} %bitcast.85), kind=kOutput, calls=%fused_computation.17 | convolution fusion | flops 678955264 | bytes 2822144 | tf_op jit(solution)/shard_map/grse,sgrd->egd/dot_general | solution.py:47
  129.6 0.0 slice-start
  129.6 0.0 copy-done
  129.6 0.0 slice-start.1
  129.6 4.3 %fusion.2 = (f32[2,2,256]{2,1,0:T(2,128)S(1)}, f32[2,1280,256,2]{2,1,3,0:T(8,128)S(1)}) fusion(f32[2,2,256]{2,1,0:T(2,128)S(1)} %get-tuple-element.17, f32[2,2,256,1280]{2,3,1,0:T(8,128)} %get-tuple-element.18, pred[256,1280]{0,1:T(8,128)(4,1)S(1)} %and_and_fusion, bf16[1280,2,128,1]{0,2,3,1:T(8,128)(2,1)S(1)} %bitcast.87, ...), kind=kOutput, calls=%fused_computation.4 | convolution fusion | flops 340786176 | bytes 11739136 | tf_op jit(solution)/shard_map/sgrd,egd->grse/dot_general | solution.py:40
  133.9 0.0 slice-done
  133.9 0.0 slice-done.1
  134.0 2.3 %fusion.4 = bf16[2,2,256,1280]{2,3,1,0:T(8,128)(2,1)S(1)} fusion(f32[2,1280,256,2]{2,1,3,0:T(8,128)S(1)} %get-tuple-element.20, f32[2,2,256]{2,1,0:T(2,128)S(1)} %get-tuple-element.19, f32[2,2,256]{2,1,0:T(2,128)S(1)} %get-tuple-element.17, f32[2,2,256,1280]{2,3,1,0:T(8,128)S(1)} %bitcast.73, pred[256,1280]{0,1:T(8,128)(4,1)} %copy-done), kind=kLoop, calls=%fused_computation.6 | loop fusion | flops 6553600 | bytes 13443072 | tf_op jit(solution)/shard_map/convert_element_type | solution.py:46
  136.2 2.1 fusion.7
  138.3 2.8 %copy.30 = f32[1,1280,256]{2,1,0:T(8,128)} copy(f32[1,1280,256]{1,2,0:T(8,128)} %bitcast.74) | data formatting | bytes 2621440 | tf_op jit(solution)/shard_map/stack;reshape | solution.py:87
  141.1 2.8 %copy.31 = f32[1,1280,256]{2,1,0:T(8,128)} copy(f32[1,1280,256]{1,2,0:T(8,128)} %bitcast.79) | data formatting | bytes 2621440 | tf_op jit(solution)/shard_map/stack;reshape | solution.py:87
  143.9 1.9 fusion.8
  145.8 1.0 fusion.20
  146.8 3.7 %collective-permute-start.4 = (bf16[2,256,256]{2,1,0:T(8,128)(2,1)}, bf16[2,256,256]{2,1,0:T(8,128)(2,1)S(1)}, u32[]{:S(2)}, u32[]{:S(2)}) collective-permute-start(bf16[2,256,256]{2,1,0:T(8,128)(2,1)} %get-tuple-element.9), channel_id=1, source_target_pairs={{16,0},{20,4},{24,8},{28,12},{32,16},{36,20},{40,24},{44,28},{48,3... | collective-permute-start | bytes 786440 | tf_op jit(solution)/shard_map/ppermute | solution.py:16
  150.5 6.0 %collective-permute-start.5 = (bf16[2,256,256]{2,1,0:T(8,128)(2,1)}, bf16[2,256,256]{2,1,0:T(8,128)(2,1)}, u32[]{:S(2)}, u32[]{:S(2)}) collective-permute-start(bf16[2,256,256]{2,1,0:T(8,128)(2,1)} %get-tuple-element.12), channel_id=1, source_target_pairs={{12,0},{16,4},{20,8},{24,12},{28,16},{32,20},{36,24},{40,28},{44,3... | collective-permute-start | bytes 786440 | tf_op jit(solution)/shard_map/ppermute | solution.py:16
  156.5 3.9 %collective-permute-start.6 = (bf16[2,256,256]{2,1,0:T(8,128)(2,1)}, bf16[2,256,256]{2,1,0:T(8,128)(2,1)}, u32[]{:S(2)}, u32[]{:S(2)}) collective-permute-start(bf16[2,256,256]{2,1,0:T(8,128)(2,1)} %get-tuple-element.11), channel_id=1, source_target_pairs={{8,0},{12,4},{16,8},{20,12},{24,16},{28,20},{32,24},{36,28},{40,32... | collective-permute-start | bytes 786440 | tf_op jit(solution)/shard_map/ppermute | solution.py:16
  160.4 4.9 %collective-permute-start.7 = (bf16[2,256,256]{2,1,0:T(8,128)(2,1)}, bf16[2,256,256]{2,1,0:T(8,128)(2,1)}, u32[]{:S(2)}, u32[]{:S(2)}) collective-permute-start(bf16[2,256,256]{2,1,0:T(8,128)(2,1)} %get-tuple-element.10), channel_id=1, source_target_pairs={{4,0},{8,4},{12,8},{16,12},{20,16},{24,20},{28,24},{32,28},{36,32}... | collective-permute-start | bytes 786440 | tf_op jit(solution)/shard_map/ppermute | solution.py:16
  165.4 1.3 convolution_multiply_fusion
  166.7 2.0 copy.32
  168.7 3.1 %collective-permute-done.4 = bf16[2,256,256]{2,1,0:T(8,128)(2,1)S(1)} collective-permute-done((bf16[2,256,256]{2,1,0:T(8,128)(2,1)}, bf16[2,256,256]{2,1,0:T(8,128)(2,1)S(1)}, u32[]{:S(2)}, u32[]{:S(2)}) %collective-permute-start.4) | collective-permute-done | bytes 262176 | tf_op jit(solution)/shard_map/ppermute | solution.py:16
  171.8 3.4 %collective-permute-done.5 = bf16[2,256,256]{2,1,0:T(8,128)(2,1)} collective-permute-done((bf16[2,256,256]{2,1,0:T(8,128)(2,1)}, bf16[2,256,256]{2,1,0:T(8,128)(2,1)}, u32[]{:S(2)}, u32[]{:S(2)}) %collective-permute-start.5) | collective-permute-done | bytes 262176 | tf_op jit(solution)/shard_map/ppermute | solution.py:16
  175.3 16.2 %collective-permute-done.6 = bf16[2,256,256]{2,1,0:T(8,128)(2,1)} collective-permute-done((bf16[2,256,256]{2,1,0:T(8,128)(2,1)}, bf16[2,256,256]{2,1,0:T(8,128)(2,1)}, u32[]{:S(2)}, u32[]{:S(2)}) %collective-permute-start.6) | collective-permute-done | bytes 262176 | tf_op jit(solution)/shard_map/ppermute | solution.py:16
  191.5 12.5 %collective-permute-done.7 = bf16[2,256,256]{2,1,0:T(8,128)(2,1)} collective-permute-done((bf16[2,256,256]{2,1,0:T(8,128)(2,1)}, bf16[2,256,256]{2,1,0:T(8,128)(2,1)}, u32[]{:S(2)}, u32[]{:S(2)}) %collective-permute-start.7) | collective-permute-done | bytes 262176 | tf_op jit(solution)/shard_map/ppermute | solution.py:16
  204.0 1.4 fusion.15
  205.4 0.8 slice_bitcast_fusion
  (10 shorter events, 0.1 us)
Async XLA Ops:
  7.2 113.2 %all-gather.2.cloned.1.call-start = ((), (), s32[]{:S(2)}) async-start(), calls=%async_computation | async-start | bytes 3440640 | tf_op jit(solution)/shard_map/all_gather | solution.py:69
  10.0 36.5 %collective-permute-start = (bf16[2,256,256]{1,2,0:T(8,128)(2,1)S(1)}, bf16[2,256,256]{1,2,0:T(8,128)(2,1)S(1)}, u32[]{:S(2)}, u32[]{:S(2)}) collective-permute-start(bf16[2,256,256]{1,2,0:T(8,128)(2,1)S(1)} %pad_maximum_fusion.1), channel_id=1, source_target_pairs={{0,16},{4,20},{8,24},{12,28},{16,32},{20,36},{24,40},{28,44},{32,4... | collective-permute-start | bytes 786440 | tf_op jit(solution)/shard_map/ppermute | solution.py:16
  24.5 24.2 %collective-permute-start.1 = (bf16[2,256,256]{1,2,0:T(8,128)(2,1)S(1)}, bf16[2,256,256]{1,2,0:T(8,128)(2,1)S(1)}, u32[]{:S(2)}, u32[]{:S(2)}) collective-permute-start(bf16[2,256,256]{1,2,0:T(8,128)(2,1)S(1)} %pad_maximum_fusion.1), channel_id=1, source_target_pairs={{0,12},{4,16},{8,20},{12,24},{16,28},{20,32},{24,36},{28,40},{32,4... | collective-permute-start | bytes 786440 | tf_op jit(solution)/shard_map/ppermute | solution.py:16
  26.4 42.4 %collective-permute-start.2 = (bf16[2,256,256]{1,2,0:T(8,128)(2,1)S(1)}, bf16[2,256,256]{1,2,0:T(8,128)(2,1)S(1)}, u32[]{:S(2)}, u32[]{:S(2)}) collective-permute-start(bf16[2,256,256]{1,2,0:T(8,128)(2,1)S(1)} %pad_maximum_fusion.1), channel_id=1, source_target_pairs={{0,8},{4,12},{8,16},{12,20},{16,24},{20,28},{24,32},{28,36},{32,40... | collective-permute-start | bytes 786440 | tf_op jit(solution)/shard_map/ppermute | solution.py:16
  30.8 46.2 %collective-permute-start.3 = (bf16[2,256,256]{1,2,0:T(8,128)(2,1)S(1)}, bf16[2,256,256]{1,2,0:T(8,128)(2,1)S(1)}, u32[]{:S(2)}, u32[]{:S(2)}) collective-permute-start(bf16[2,256,256]{1,2,0:T(8,128)(2,1)S(1)} %pad_maximum_fusion.1), channel_id=1, source_target_pairs={{0,4},{4,8},{8,12},{12,16},{16,20},{20,24},{24,28},{28,32},{32,36}... | collective-permute-start | bytes 786440 | tf_op jit(solution)/shard_map/ppermute | solution.py:16
  37.2 92.4 %copy-start = (pred[256,1280]{0,1:T(8,128)(4,1)}, pred[256,1280]{0,1:T(8,128)(4,1)S(1)}, u32[]{:S(2)}) copy-start(pred[256,1280]{0,1:T(8,128)(4,1)S(1)} %and_and_fusion) | copy-start | bytes 983044
  129.6 4.3 %slice-start = ((s8[5242880]{0:T(1024)(128)(4,1)}), s8[4194304]{0:T(1024)(128)(4,1)S(1)}, s32[]{:S(2)}) async-start(s8[5242880]{0:T(1024)(128)(4,1)} %bitcast.72), calls=%async_computation.1 | async-start | bytes 8388608
  129.6 4.3 %slice-start.1 = ((s8[5242880]{0:T(1024)(128)(4,1)}), s8[1048576]{0:T(1024)(128)(4,1)S(1)}, s32[]{:S(2)}) async-start(s8[5242880]{0:T(1024)(128)(4,1)} %bitcast.72), calls=%async_computation.2 | async-start | bytes 2097152
  146.8 25.1 %collective-permute-start.4 = (bf16[2,256,256]{2,1,0:T(8,128)(2,1)}, bf16[2,256,256]{2,1,0:T(8,128)(2,1)S(1)}, u32[]{:S(2)}, u32[]{:S(2)}) collective-permute-start(bf16[2,256,256]{2,1,0:T(8,128)(2,1)} %get-tuple-element.9), channel_id=1, source_target_pairs={{16,0},{20,4},{24,8},{28,12},{32,16},{36,20},{40,24},{44,28},{48,3... | collective-permute-start | bytes 786440 | tf_op jit(solution)/shard_map/ppermute | solution.py:16
  150.5 24.8 %collective-permute-start.5 = (bf16[2,256,256]{2,1,0:T(8,128)(2,1)}, bf16[2,256,256]{2,1,0:T(8,128)(2,1)}, u32[]{:S(2)}, u32[]{:S(2)}) collective-permute-start(bf16[2,256,256]{2,1,0:T(8,128)(2,1)} %get-tuple-element.12), channel_id=1, source_target_pairs={{12,0},{16,4},{20,8},{24,12},{28,16},{32,20},{36,24},{40,28},{44,3... | collective-permute-start | bytes 786440 | tf_op jit(solution)/shard_map/ppermute | solution.py:16
  156.5 35.0 %collective-permute-start.6 = (bf16[2,256,256]{2,1,0:T(8,128)(2,1)}, bf16[2,256,256]{2,1,0:T(8,128)(2,1)}, u32[]{:S(2)}, u32[]{:S(2)}) collective-permute-start(bf16[2,256,256]{2,1,0:T(8,128)(2,1)} %get-tuple-element.11), channel_id=1, source_target_pairs={{8,0},{12,4},{16,8},{20,12},{24,16},{28,20},{32,24},{36,28},{40,32... | collective-permute-start | bytes 786440 | tf_op jit(solution)/shard_map/ppermute | solution.py:16
  160.4 43.6 %collective-permute-start.7 = (bf16[2,256,256]{2,1,0:T(8,128)(2,1)}, bf16[2,256,256]{2,1,0:T(8,128)(2,1)}, u32[]{:S(2)}, u32[]{:S(2)}) collective-permute-start(bf16[2,256,256]{2,1,0:T(8,128)(2,1)} %get-tuple-element.10), channel_id=1, source_target_pairs={{4,0},{8,4},{12,8},{16,12},{20,16},{24,20},{28,24},{32,28},{36,32}... | collective-permute-start | bytes 786440 | tf_op jit(solution)/shard_map/ppermute | solution.py:16
Sparse Core Ops, SparseCore 0:
  10.4 109.9 all-gather.1
where the time goes:
time: 214 us; the launch traced here: 213 us
  waiting for transfers between devices  113 us (53%)
  starting transfers between devices  44.8 us (21%)
  matrix products  21.6 us (10%)
  between operations  14.3 us (7%)
  local copies, waits for them, and re-layouts  13 us (6%)
  other arithmetic  6.59 us (3%)
    ppermute x8, waiting for transfers between devices, passed_along(): return lax.ppermute(block, axis, route)  73.8 us
    ppermute x8, starting transfers between devices, passed_along(): return lax.ppermute(block, axis, route)  44.8 us
    all_gather x1, waiting for transfers between devices, on_device(): lax.all_gather(grad_out, 'tp', axis=0, tiled=True)  38.4 us
    another operation x2, local copies, waits for them, and re-layouts, on_device(): span_grads = jnp.stack([grad_key, grad_value])  5.6 us
    dot_general x1, matrix products, on_device(): lax.dot_general(lax.all_gather(grad_out, 'tp', axis=0, tiled=True), out_w...  5.01 us
    sub x1, matrix products, band_grads(): weights = jnp.where(allowed, jnp.exp(scores - row_max), 0.0)  4.83 us
    dot_general x1, matrix products, band_grads(): jnp.einsum('sgrd,egd->grse', dout_heads, value_heads, preferred_element_t...  4.3 us
  transfers between devices with their start and end apart: 9, of which 9 were waited for; matrix products, arithmetic and copies ran while one was open for 6% of the time, Pallas kernels for 0%

commit v1 on v0

v1 whole, which is shorter than its diff:
```python
import functools

import jax
import jax.numpy as jnp
from jax import lax
from jax.experimental import pallas as pl
from jax.experimental.pallas import tpu as pltpu
from jax.sharding import PartitionSpec as P

HD = 128
WIN = 1024
SCALE = 168.0 ** (-0.5)
LOG2E = 1.4426950408889634
NEG = -1e30
MESH = pl.DeviceIdType.MESH
ZHI, ZLO = 3, 4
F32 = jnp.float32
BF16 = jnp.bfloat16

ROWS = (
    ((96, 0, 160), (0, 160, 96), -1),
    ((32, 0, 224), (0, 224, 32), -1),
    ((0, 32, 224), (224, 0, 32), 1),
    ((0, 96, 160), (160, 0, 96), 1),
)


def dot_nt(a, b):
    return lax.dot_general(a, b, (((1,), (1,)), ((), ())), preferred_element_type=F32)


def dot_nn(a, b):
    return lax.dot_general(a, b, (((1,), (0,)), ((), ())), preferred_element_type=F32)


def dot_tn(a, b):
    return lax.dot_general(a, b, (((0,), (0,)), ((), ())), preferred_element_type=F32)


def kernel(
    chips, q_in, k_in, v_in, g_in, w_in, gq_out, gk_out, gv_out,
    main, relay, wbuf, ybuf, dobuf, qbuf, kvbuf, pbuf, dpbuf, dsbuf, stats,
    gsend, grecv, ownf, pbase, ost, dqx,
    loc, ag_s, ag_r, kv_s, kv_r, q_s, q_r, do_s, do_r, gr_s, gr_r, fin_s, fin_r,
):
    ctx = lax.axis_index("ctx")
    k = lax.axis_index("tp")
    e = lax.rem(ctx, 2)
    f = 1 - e
    c = ctx // 2
    r = c // ZHI
    zh = lax.rem(c, ZHI)
    z = zh * ZLO + k
    nz = ZHI * ZLO

    def plane(d):
        zz = lax.rem(z + d + nz, nz)
        return (((r * ZHI + zz // ZLO) * 2 + e), lax.rem(zz, ZLO))

    def group(d, core):
        return ((r * ZHI + lax.rem(zh + d + ZHI, ZHI)) * 2 + core, k)

    def chip(d, core):
        return (lax.rem(c + d + chips, chips) * 2 + core, k)

    partner = (c * 2 + f, k)

    def remote(src, dst, ss, rs, dev):
        return pltpu.make_async_remote_copy(
            src_ref=src, dst_ref=dst, send_sem=ss, recv_sem=rs, device_id=dev, device_id_type=MESH
        )

    def arrive(dst, rs):
        remote(dst, dst, rs, rs, partner).wait_recv()

    def lane(i, n):
        return pl.ds(pl.multiple_of(i * n, n), n)

    local = [
        pltpu.make_async_copy(g_in, main.at[64:128], loc.at[0]),
        pltpu.make_async_copy(w_in, wbuf, loc.at[1]),
        pltpu.make_async_copy(k_in.at[:, lane(e, 128)], kvbuf.at[0, 4 + e], loc.at[2]),
        pltpu.make_async_copy(v_in.at[:, lane(e, 128)], kvbuf.at[1, 4 + e], loc.at[3]),
        pltpu.make_async_copy(q_in.at[:, lane(e, 256)], qbuf.at[e], loc.at[4]),
    ]
    for copy in local:
        copy.start()

    barrier = pltpu.get_barrier_semaphore()

    def greet(dev):
        pl.semaphore_signal(barrier, inc=1, device_id=dev, device_id_type=MESH)

    back = jnp.where(k < 2, 1, -1)
    greet(partner)
    greet(plane(1))
    greet(plane(-1))
    for core in range(2):
        greet(group(back, core))
        for d in (1, 2, -1, -2):
            greet(chip(d, core))
    pl.semaphore_wait(barrier, 13)

    sends = []

    def send(*args):
        copy = remote(*args)
        copy.start()
        sends.append(copy)

    send(g_in.at[32:64], main.at[32:64], ag_s.at[0], ag_r.at[0], plane(1))
    send(g_in.at[0:32], main.at[128:160], ag_s.at[1], ag_r.at[1], plane(-1))
    send(g_in.at[0:32], main.at[0:32], ag_s.at[2], ag_r.at[2], plane(1))
    send(g_in.at[32:64], main.at[160:192], ag_s.at[3], ag_r.at[3], plane(-1))
    send(q_in.at[:, lane(f, 256)], qbuf.at[e], q_s.at[0], q_r.at[0], partner)
    send(k_in.at[:, lane(f, 128)], kvbuf.at[0, 4 + e], kv_s.at[0], kv_r.at[0], partner)
    send(v_in.at[:, lane(f, 128)], kvbuf.at[1, 4 + e], kv_s.at[1], kv_r.at[1], partner)
    arrive(main.at[32:64], ag_r.at[0])
    send(main.at[32:64], relay.at[0:32], ag_s.at[4], ag_r.at[4], plane(1))
    arrive(main.at[128:160], ag_r.at[1])
    send(main.at[128:160], relay.at[32:64], ag_s.at[5], ag_r.at[5], plane(-1))
    for d in (1, 2):
        for core in range(2):
            for which, src in ((0, k_in), (1, v_in)):
                slot = 2 + (d - 1) * 4 + which
                send(
                    src.at[:, 128 * core : 128 * core + 128],
                    kvbuf.at[which, 4 - 2 * d + e],
                    kv_s.at[slot + 2 * core],
                    kv_r.at[slot + 2 * e],
                    chip(d, core),
                )

    for copy in local:
        copy.wait()
    arrive(main.at[0:32], ag_r.at[2])
    arrive(main.at[160:192], ag_r.at[3])
    for h in range(2):
        ybuf[h, 32:224] = dot_nt(main[...], wbuf[256 * h : 256 * h + 256]).astype(BF16)
    arrive(relay.at[0:32], ag_r.at[4])
    arrive(relay.at[32:64], ag_r.at[5])
    for h in range(2):
        ends = dot_nt(relay[...], wbuf[256 * h : 256 * h + 256]).astype(BF16)
        ybuf[h, 0:32] = ends[0:32]
        ybuf[h, 224:256] = ends[32:64]

    for case, (kept, moved, way) in enumerate(ROWS):
        src, home, count = kept
        msrc, mhome, mcount = moved

        def rows_out():
            copies = [
                remote(
                    ybuf.at[core, msrc : msrc + mcount],
                    dobuf.at[e, mhome : mhome + mcount],
                    do_s.at[1 + core],
                    do_r.at[1 + e],
                    group(way, core),
                )
                for core in range(2)
            ]
            copies.append(
                remote(
                    ybuf.at[f, src : src + count],
                    dobuf.at[e, home : home + count],
                    do_s.at[0],
                    do_r.at[0],
                    partner,
                )
            )
            return copies

        @pl.when(k == case)
        def _():
            for copy in rows_out():
                copy.start()
            own = pltpu.make_async_copy(
                ybuf.at[e, src : src + count], dobuf.at[e, home : home + count], loc.at[5]
            )
            own.start()
            own.wait()
            arrive(dobuf.at[f, home : home + count], do_r.at[0])
            for core in range(2):
                arrive(dobuf.at[core, mhome : mhome + mcount], do_r.at[1 + core])
            for copy in rows_out():
                copy.wait_send()

    arrive(qbuf.at[f], q_r.at[0])
    for which in range(2):
        arrive(kvbuf.at[which, 4 + f], kv_r.at[which])
    for d in (1, 2):
        for core in range(2):
            for which in range(2):
                arrive(
                    kvbuf.at[which, 4 - 2 * d + core], kv_r.at[2 + (d - 1) * 4 + which + 2 * core]
                )

    key_row = lax.broadcasted_iota(jnp.int32, (256, 256), 0)
    query_col = lax.broadcasted_iota(jnp.int32, (256, 256), 1)
    c2 = SCALE * LOG2E

    def softmax(qb, carry):
        for head in range(2):
            n = qb * 2 + head
            cols = slice(128 * head, 128 * head + 128)
            queries = qbuf[qb, :, cols]
            dout = dobuf[qb, :, cols]
            top = jnp.full((1, 256), NEG, F32)
            for jj in range(5):
                s = dot_nt(kvbuf[0, qb + jj], queries)
                if jj == 0:
                    s = jnp.where(key_row > query_col, s, NEG)
                if jj == 4:
                    s = jnp.where(key_row <= query_col, s, NEG)
                pbuf[n, jj] = s
                there = 2 * c + qb + jj >= 4
                top = jnp.maximum(
                    top, jnp.where(there, jnp.max(s, axis=0, keepdims=True), NEG)
                )
            top = top * c2
            total = jnp.zeros((1, 256), F32)
            delta = jnp.zeros((1, 256), F32)
            for jj in range(5):
                there = 2 * c + qb + jj >= 4
                p = jnp.exp2(pbuf[n, jj] * c2 - jnp.where(there, top, -NEG))
                dp = dot_nt(kvbuf[1, qb + jj], dout)
                total = total + jnp.sum(p, axis=0, keepdims=True)
                delta = delta + jnp.sum(p * dp, axis=0, keepdims=True)
                pbuf[n, jj] = p
                dpbuf[n, jj] = dp
            inverse = 1.0 / total
            stats[n, 0:1] = inverse
            stats[n, 1:2] = delta * inverse
        return carry

    lax.fori_loop(0, 2, softmax, 0)

    def terms(j):
        dk = jnp.zeros((256, 128), F32)
        dv = jnp.zeros((256, 128), F32)
        for qb in range(2):
            jj = j - qb
            if jj < 0 or jj > 4:
                continue
            for head in range(2):
                n = qb * 2 + head
                cols = slice(128 * head, 128 * head + 128)
                p = pbuf[n, jj] * stats[n, 0:1]
                ds = (p * (dpbuf[n, jj] - stats[n, 1:2])).astype(BF16)
                dsbuf[n, jj] = ds
                dv = dv + dot_nn(p.astype(BF16), dobuf[qb, :, cols])
                dk = dk + dot_nn(ds, qbuf[qb, :, cols])
        return dk * SCALE, dv

    for j in (0, 2, 1, 3):
        dk, dv = terms(j)
        gsend[j, 0] = dk.astype(BF16)
        gsend[j, 1] = dv.astype(BF16)
        d, core = 2 - j // 2, j % 2
        send(
            gsend.at[j], grecv.at[d - 1, e], gr_s.at[j], gr_r.at[(d - 1) * 2 + e], chip(-d, core)
        )
    for core in range(2):
        dk, dv = terms(4 + core)
        ownf[core, 0] = dk
        ownf[core, 1] = dv
    send(ownf.at[f], pbase, fin_s.at[0], fin_r.at[0], partner)
    for qb in range(2):
        for head in range(2):
            n = qb * 2 + head
            dq = jnp.zeros((256, 128), F32)
            for jj in range(5):
                dq = dq + dot_tn(dsbuf[n, jj], kvbuf[0, qb + jj])
            dqx[qb, :, 128 * head : 128 * head + 128] = dq * SCALE
    send(dqx.at[f], gq_out.at[:, lane(e, 256)], fin_s.at[1], fin_r.at[1], partner)
    gq_own = pltpu.make_async_copy(dqx.at[e], gq_out.at[:, lane(e, 256)], loc.at[6])
    gq_own.start()

    for which in range(2):
        ost[e, which] = ownf[e, which]
    arrive(pbase, fin_r.at[0])
    for which in range(2):
        ost[f, which] = pbase[which]
    outs = []
    for d in (1, 2):
        for core in range(2):
            arrive(grecv.at[d - 1, core], gr_r.at[(d - 1) * 2 + core])
    for core in range(2):
        for which, out in ((0, gk_out), (1, gv_out)):
            ost[core, which] = (
                ost[core, which]
                + grecv[0, core, which].astype(F32)
                + grecv[1, core, which].astype(F32)
            )
            copy = pltpu.make_async_copy(
                ost.at[core, which],
                out.at[:, 128 * core : 128 * core + 128],
                loc.at[7 + 2 * core + which],
            )
            copy.start()
            outs.append(copy)
    arrive(gq_out.at[:, lane(f, 256)], fin_r.at[1])
    gq_own.wait()
    for copy in outs:
        copy.wait()
    for copy in sends:
        copy.wait_send()


def on_device(chips, q, k, v, g, w):
    rows, width = q.shape
    kv_width = k.shape[1]
    model = g.shape[1]
    any_spec = pl.BlockSpec(memory_space=pl.ANY)
    dma = pltpu.SemaphoreType.DMA
    vmem = pltpu.VMEM
    return pl.pallas_call(
        functools.partial(kernel, chips),
        out_shape=(
            jax.ShapeDtypeStruct((rows, width), F32),
            jax.ShapeDtypeStruct((rows, kv_width), F32),
            jax.ShapeDtypeStruct((rows, kv_width), F32),
        ),
        in_specs=[any_spec] * 5,
        out_specs=[any_spec] * 3,
        scratch_shapes=[
            vmem((192, model), BF16),
            vmem((64, model), BF16),
            vmem((512, model), BF16),
            vmem((2, 256, 256), BF16),
            vmem((2, 256, 256), BF16),
            vmem((2, 256, 256), BF16),
            vmem((2, 6, 256, 128), BF16),
            vmem((4, 5, 256, 256), F32),
            vmem((4, 5, 256, 256), F32),
            vmem((4, 5, 256, 256), BF16),
            vmem((4, 8, 256), F32),
            vmem((4, 2, 256, 128), BF16),
            vmem((2, 2, 2, 256, 128), BF16),
            vmem((2, 2, 256, 128), F32),
            vmem((2, 256, 128), F32),
            vmem((2, 2, 256, 128), F32),
            vmem((2, 256, 256), F32),
            dma((12,)),
            dma((6,)),
            dma((6,)),
            dma((10,)),
            dma((10,)),
            dma((1,)),
            dma((1,)),
            dma((3,)),
            dma((3,)),
            dma((4,)),
            dma((4,)),
            dma((2,)),
            dma((2,)),
        ],
        compiler_params=pltpu.CompilerParams(
            collective_id=0, has_side_effects=True, vmem_limit_bytes=60 * 1024 * 1024
        ),
        name="band_grads",
    )(q, k, v, g, w)


def solution(mesh):
    in_specs = (
        P("ctx", "tp"),
        P("ctx", "tp"),
        P("ctx", "tp"),
        P(("ctx", "tp"), None),
        P("tp", None),
    )
    out_specs = (P("ctx", "tp"), P("ctx", "tp"), P("ctx", "tp"))
    chips = mesh.shape["ctx"] // 2
    return jax.shard_map(
        functools.partial(on_device, chips),
        mesh=mesh,
        in_specs=in_specs,
        out_specs=out_specs,
        check_vma=False,
    )
```

time: 214 us -> 106 us (0.50)
  the two profiles are of different devices: /device:TPU:56 before, /device:TPU:7 now
where the time goes in v1:
time: 106 us
  Pallas kernels  100 us (94%)
  local copies, waits for them, and re-layouts  5.21 us (5%)
    pallas_call x1, Pallas kernels, on_device(): pl.pallas_call(functools.partial(kernel, chips), out_shape=(jax.ShapeDtyp...  100 us
    unnamed x3, local copies, waits for them, and re-layouts  5.21 us

profile of v1, /device:TPU:7, one launch (start us, length us, event | category | flops | bytes accessed | tf_op | source)
XLA Modules:
  0.0 106.2 jit_solution(10216215856840666833)
XLA Ops:
  0.6 100.3 %band_grads.1 = (f32[256,512]{1,0:T(8,128)}, f32[256,256]{1,0:T(8,128)}, f32[256,256]{1,0:T(8,128)}) custom-call(bf16[256,512]{1,0:T(8,128)(2,1)} %q_in.1, bf16[256,256]{1,0:T(8,128)(2,1)} %k_in.1, bf16[256,256]{1,0:T(8,128)(2,1)} %v_in.1, bf16[64,5376]{1,0:T(8,128)(2,1)} %g_in.1, bf16[512,5376]{1,0:T(8,128)(2,1)} %w_in.1), custom_call_target="tpu_custom_call" | custom-call | tf_op jit(solution)/shard_map/band_grads/pallas_call | solution.py:317
  101.0 1.9 %copy.11 = f32[256,512]{1,0:T(8,128)} copy(f32[256,512]{1,0:T(8,128)} %get-tuple-element.6) | data formatting | bytes 1048576
  102.8 1.7 %copy.12 = f32[256,256]{1,0:T(8,128)} copy(f32[256,256]{1,0:T(8,128)} %get-tuple-element.7) | data formatting | bytes 524288
  104.5 1.7 %copy.13 = f32[256,256]{1,0:T(8,128)} copy(f32[256,256]{1,0:T(8,128)} %get-tuple-element.8) | data formatting | bytes 524288

commit v2 on v1

--- a/solution.py
+++ b/solution.py
@@ -38,10 +38,10 @@
 
 
 def kernel(
-    chips, q_in, k_in, v_in, g_in, w_in, gq_out, gk_out, gv_out,
+    chips, q_in, k_in, v_in, g_in, w_in, gq_out, base, grecv,
     main, relay, wbuf, ybuf, dobuf, qbuf, kvbuf, pbuf, dpbuf, dsbuf, stats,
-    gsend, grecv, ownf, pbase, ost, dqx,
-    loc, ag_s, ag_r, kv_s, kv_r, q_s, q_r, do_s, do_r, gr_s, gr_r, fin_s, fin_r,
+    gsend, ownf, dqx,
+    ready, loc, ag_s, ag_r, kv_s, kv_r, q_s, q_r, do_s, do_r, gr_s, gr_r, fin_s, fin_r,
 ):
     ctx = lax.axis_index("ctx")
     k = lax.axis_index("tp")
@@ -53,9 +53,9 @@
     z = zh * ZLO + k
     nz = ZHI * ZLO
 
-    def plane(d):
+    def plane(d, core):
         zz = lax.rem(z + d + nz, nz)
-        return (((r * ZHI + zz // ZLO) * 2 + e), lax.rem(zz, ZLO))
+        return (((r * ZHI + zz // ZLO) * 2 + core), lax.rem(zz, ZLO))
 
     def group(d, core):
         return ((r * ZHI + lax.rem(zh + d + ZHI, ZHI)) * 2 + core, k)
@@ -93,13 +93,11 @@
 
     back = jnp.where(k < 2, 1, -1)
     greet(partner)
-    greet(plane(1))
-    greet(plane(-1))
-    for core in range(2):
-        greet(group(back, core))
-        for d in (1, 2, -1, -2):
-            greet(chip(d, core))
-    pl.semaphore_wait(barrier, 13)
+    greet(plane(1, 1))
+    greet(plane(-1, 1))
+    greet(group(back, 0))
+    for d in (1, 2, -1, -2):
+        greet(chip(d, 0))
 
     sends = []
 
@@ -108,17 +106,35 @@
         copy.start()
         sends.append(copy)
 
-    send(g_in.at[32:64], main.at[32:64], ag_s.at[0], ag_r.at[0], plane(1))
-    send(g_in.at[0:32], main.at[128:160], ag_s.at[1], ag_r.at[1], plane(-1))
-    send(g_in.at[0:32], main.at[0:32], ag_s.at[2], ag_r.at[2], plane(1))
-    send(g_in.at[32:64], main.at[160:192], ag_s.at[3], ag_r.at[3], plane(-1))
+    @pl.when(e == 1)
+    def _():
+        pl.semaphore_wait(barrier, 5)
+        pl.semaphore_signal(ready.at[0], inc=1, device_id=partner, device_id_type=MESH)
+
+    @pl.when(e == 0)
+    def _():
+        pl.semaphore_wait(ready.at[0], 1)
+
+    send(g_in.at[32:64], main.at[32:64], ag_s.at[0], ag_r.at[0], plane(1, e))
+    send(g_in.at[0:32], main.at[128:160], ag_s.at[1], ag_r.at[1], plane(-1, e))
+    send(g_in.at[0:32], main.at[0:32], ag_s.at[2], ag_r.at[2], plane(1, e))
+    send(g_in.at[32:64], main.at[160:192], ag_s.at[3], ag_r.at[3], plane(-1, e))
     send(q_in.at[:, lane(f, 256)], qbuf.at[e], q_s.at[0], q_r.at[0], partner)
     send(k_in.at[:, lane(f, 128)], kvbuf.at[0, 4 + e], kv_s.at[0], kv_r.at[0], partner)
     send(v_in.at[:, lane(f, 128)], kvbuf.at[1, 4 + e], kv_s.at[1], kv_r.at[1], partner)
     arrive(main.at[32:64], ag_r.at[0])
-    send(main.at[32:64], relay.at[0:32], ag_s.at[4], ag_r.at[4], plane(1))
+    send(main.at[32:64], relay.at[0:32], ag_s.at[4], ag_r.at[4], plane(1, e))
     arrive(main.at[128:160], ag_r.at[1])
-    send(main.at[128:160], relay.at[32:64], ag_s.at[5], ag_r.at[5], plane(-1))
+    send(main.at[128:160], relay.at[32:64], ag_s.at[5], ag_r.at[5], plane(-1, e))
+    @pl.when(e == 0)
+    def _():
+        pl.semaphore_wait(barrier, 11)
+        pl.semaphore_signal(ready.at[1], inc=1, device_id=partner, device_id_type=MESH)
+
+    @pl.when(e == 1)
+    def _():
+        pl.semaphore_wait(ready.at[1], 1)
+
     for d in (1, 2):
         for core in range(2):
             for which, src in ((0, k_in), (1, v_in)):
@@ -264,7 +280,9 @@
         dk, dv = terms(4 + core)
         ownf[core, 0] = dk
         ownf[core, 1] = dv
-    send(ownf.at[f], pbase, fin_s.at[0], fin_r.at[0], partner)
+    send(ownf.at[f], base.at[e], fin_s.at[0], fin_r.at[0], partner)
+    kept = [pltpu.make_async_copy(ownf.at[e], base.at[e], loc.at[7])]
+    kept[0].start()
     for qb in range(2):
         for head in range(2):
             n = qb * 2 + head
@@ -273,38 +291,42 @@
                 dq = dq + dot_tn(dsbuf[n, jj], kvbuf[0, qb + jj])
             dqx[qb, :, 128 * head : 128 * head + 128] = dq * SCALE
     send(dqx.at[f], gq_out.at[:, lane(e, 256)], fin_s.at[1], fin_r.at[1], partner)
-    gq_own = pltpu.make_async_copy(dqx.at[e], gq_out.at[:, lane(e, 256)], loc.at[6])
-    gq_own.start()
-
-    for which in range(2):
-        ost[e, which] = ownf[e, which]
-    arrive(pbase, fin_r.at[0])
-    for which in range(2):
-        ost[f, which] = pbase[which]
-    outs = []
+    kept.append(pltpu.make_async_copy(dqx.at[e], gq_out.at[:, lane(e, 256)], loc.at[6]))
+    kept[1].start()
+    for copy in kept:
+        copy.wait()
+    arrive(base.at[f], fin_r.at[0])
+    arrive(gq_out.at[:, lane(f, 256)], fin_r.at[1])
     for d in (1, 2):
         for core in range(2):
             arrive(grecv.at[d - 1, core], gr_r.at[(d - 1) * 2 + core])
-    for core in range(2):
-        for which, out in ((0, gk_out), (1, gv_out)):
-            ost[core, which] = (
-                ost[core, which]
-                + grecv[0, core, which].astype(F32)
-                + grecv[1, core, which].astype(F32)
+    for copy in sends:
+        copy.wait_send()
+
+
+def finish(gq_in, base_in, grecv_in, gq_out, gk_out, gv_out, gq, base, grecv, ost, sems):
+    loads = [
+        pltpu.make_async_copy(base_in, base, sems.at[0]),
+        pltpu.make_async_copy(grecv_in, grecv, sems.at[1]),
+        pltpu.make_async_copy(gq_in, gq, sems.at[2]),
+    ]
+    for copy in loads:
+        copy.start()
+    loads[2].wait()
+    outs = [pltpu.make_async_copy(gq, gq_out, sems.at[3])]
+    outs[0].start()
+    loads[0].wait()
+    loads[1].wait()
+    for which, out in ((0, gk_out), (1, gv_out)):
+        for h in range(2):
+            ost[which, :, 128 * h : 128 * h + 128] = (
+                base[h, which] + grecv[0, h, which].astype(F32) + grecv[1, h, which].astype(F32)
             )
-            copy = pltpu.make_async_copy(
-                ost.at[core, which],
-                out.at[:, 128 * core : 128 * core + 128],
-                loc.at[7 + 2 * core + which],
-            )
-            copy.start()
-            outs.append(copy)
-    arrive(gq_out.at[:, lane(f, 256)], fin_r.at[1])
-    gq_own.wait()
+        copy = pltpu.make_async_copy(ost.at[which], out, sems.at[4 + which])
+        copy.start()
+        outs.append(copy)
     for copy in outs:
         copy.wait()
-    for copy in sends:
-        copy.wait_send()
 
 
 def on_device(chips, q, k, v, g, w):
@@ -314,12 +336,12 @@
     any_spec = pl.BlockSpec(memory_space=pl.ANY)
     dma = pltpu.SemaphoreType.DMA
     vmem = pltpu.VMEM
-    return pl.pallas_call(
+    gq, base, grecv = pl.pallas_call(
         functools.partial(kernel, chips),
         out_shape=(
             jax.ShapeDtypeStruct((rows, width), F32),
-            jax.ShapeDtypeStruct((rows, kv_width), F32),
-            jax.ShapeDtypeStruct((rows, kv_width), F32),
+            jax.ShapeDtypeStruct((2, 2, 256, 128), F32),
+            jax.ShapeDtypeStruct((2, 2, 2, 256, 128), BF16),
         ),
         in_specs=[any_spec] * 5,
         out_specs=[any_spec] * 3,
@@ -336,11 +358,9 @@
             vmem((4, 5, 256, 256), BF16),
             vmem((4, 8, 256), F32),
             vmem((4, 2, 256, 128), BF16),
-            vmem((2, 2, 2, 256, 128), BF16),
-            vmem((2, 2, 256, 128), F32),
-            vmem((2, 256, 128), F32),
             vmem((2, 2, 256, 128), F32),
             vmem((2, 256, 256), F32),
+            pltpu.SemaphoreType.REGULAR((2,)),
             dma((12,)),
             dma((6,)),
             dma((6,)),
@@ -360,6 +380,24 @@
         ),
         name="band_grads",
     )(q, k, v, g, w)
+    return pl.pallas_call(
+        finish,
+        out_shape=(
+            jax.ShapeDtypeStruct((rows, width), F32),
+            jax.ShapeDtypeStruct((rows, kv_width), F32),
+            jax.ShapeDtypeStruct((rows, kv_width), F32),
+        ),
+        in_specs=[any_spec] * 3,
+        out_specs=[any_spec] * 3,
+        scratch_shapes=[
+            vmem((rows, width), F32),
+            vmem((2, 2, 256, 128), F32),
+            vmem((2, 2, 2, 256, 128), BF16),
+            vmem((2, rows, kv_width), F32),
+            dma((6,)),
+        ],
+        name="finish",
+    )(gq, base, grecv)
 
 
 def solution(mesh):

time: 106 us -> 95.2 us (0.90); the launches traced: 106 us -> 94.3 us
  Pallas kernels: 100 us -> 93.7 us
  local copies, waits for them, and re-layouts: 5.21 us -> 0 us
    pallas_call x1, Pallas kernels: 100 us -> 91.3 us  [on_device(): pl.pallas_call(functools.partial(kernel, chips), out_shape=(jax.ShapeDtyp...]
    unnamed x3 -> x0, local copies, waits for them, and re-layouts: 5.21 us -> none
    pallas_call x0 -> x1, Pallas kernels: none -> 2.37 us  [on_device(): pl.pallas_call(finish, out_shape=(jax.ShapeDtypeStruct((rows, width), F32...]
where the time goes in v2:
time: 95.2 us; the launch traced here: 94.3 us
  Pallas kernels  93.7 us (98%)
    pallas_call x1, Pallas kernels, on_device(): pl.pallas_call(functools.partial(kernel, chips), out_shape=(jax.ShapeDtyp...  91.3 us
    pallas_call x1, Pallas kernels, on_device(): pl.pallas_call(finish, out_shape=(jax.ShapeDtypeStruct((rows, width), F32...  2.37 us

profile of v2, /device:TPU:7, one launch (start us, length us, event | category | flops | bytes accessed | tf_op | source)
XLA Modules:
  0.0 94.3 jit_solution(6416930098391929409)
XLA Ops:
  0.6 91.3 %band_grads.1 = (f32[256,512]{1,0:T(8,128)}, f32[2,2,256,128]{3,2,1,0:T(8,128)}, bf16[2,2,2,256,128]{4,3,2,1,0:T(8,128)(2,1)}) custom-call(bf16[256,512]{1,0:T(8,128)(2,1)} %q_in.1, bf16[256,256]{1,0:T(8,128)(2,1)} %k_in.1, bf16[256,256]{1,0:T(8,128)(2,1)} %v_in.1, bf16[64,5376]{1,0:T(8,128)(2,1)} %g_in.1, bf16[512,5376]{1,0:T(8,128)(2,1)} %w_in.1), custom_call_target="tpu_custom_call" | custom-call | tf_op jit(solution)/shard_map/band_grads/pallas_call | solution.py:339
  91.9 2.4 %finish.1 = (f32[256,512]{1,0:T(8,128)}, f32[256,256]{1,0:T(8,128)}, f32[256,256]{1,0:T(8,128)}) custom-call(f32[256,512]{1,0:T(8,128)} %get-tuple-element.6.gq_in, f32[2,2,256,128]{3,2,1,0:T(8,128)} %get-tuple-element.7.base_in, bf16[2,2,2,256,128]{4,3,2,1,0:T(8,128)(2,1)} %get-tuple-element.8.grecv_in), custom_call_target="tpu_custom_call" | custom-call | tf_op jit(solution)/shard_map/finish/pallas_call | solution.py:383

commit v3 on v2

--- a/solution.py
+++ b/solution.py
@@ -126,6 +126,7 @@
     send(main.at[32:64], relay.at[0:32], ag_s.at[4], ag_r.at[4], plane(1, e))
     arrive(main.at[128:160], ag_r.at[1])
     send(main.at[128:160], relay.at[32:64], ag_s.at[5], ag_r.at[5], plane(-1, e))
+
     @pl.when(e == 0)
     def _():
         pl.semaphore_wait(barrier, 11)
@@ -135,17 +136,24 @@
     def _():
         pl.semaphore_wait(ready.at[1], 1)
 
-    for d in (1, 2):
-        for core in range(2):
+    passed = []
+    for core in range(2):
+        for d in (1, 2):
             for which, src in ((0, k_in), (1, v_in)):
                 slot = 2 + (d - 1) * 4 + which
-                send(
+                passed.append(remote(
                     src.at[:, 128 * core : 128 * core + 128],
                     kvbuf.at[which, 4 - 2 * d + e],
                     kv_s.at[slot + 2 * core],
                     kv_r.at[slot + 2 * e],
                     chip(d, core),
-                )
+                ))
+
+
+    @pl.when((k == 0) | (k == 2) | (k == 3))
+    def _():
+        for copy in passed:
+            copy.start()
 
     for copy in local:
         copy.wait()
@@ -160,46 +168,47 @@
         ybuf[h, 0:32] = ends[0:32]
         ybuf[h, 224:256] = ends[32:64]
 
-    for case, (kept, moved, way) in enumerate(ROWS):
-        src, home, count = kept
-        msrc, mhome, mcount = moved
-
-        def rows_out():
-            copies = [
-                remote(
-                    ybuf.at[core, msrc : msrc + mcount],
-                    dobuf.at[e, mhome : mhome + mcount],
-                    do_s.at[1 + core],
-                    do_r.at[1 + e],
-                    group(way, core),
-                )
-                for core in range(2)
-            ]
-            copies.append(
-                remote(
-                    ybuf.at[f, src : src + count],
-                    dobuf.at[e, home : home + count],
-                    do_s.at[0],
-                    do_r.at[0],
-                    partner,
-                )
+    def rows_out(case):
+        (src, home, count), (msrc, mhome, mcount), way = ROWS[case]
+        copies = [
+            remote(
+                ybuf.at[core, msrc : msrc + mcount],
+                dobuf.at[e, mhome : mhome + mcount],
+                do_s.at[1 + core],
+                do_r.at[1 + e],
+                group(way, core),
             )
-            return copies
+            for core in range(2)
+        ]
+        copies.append(
+            remote(
+                ybuf.at[f, src : src + count],
+                dobuf.at[e, home : home + count],
+                do_s.at[0],
+                do_r.at[0],
+                partner,
+            )
+        )
+        copies.append(
+            pltpu.make_async_copy(
+                ybuf.at[e, src : src + count], dobuf.at[e, home : home + count], loc.at[5]
+            )
+        )
+        return copies
+
+    for case in range(ZLO):
 
         @pl.when(k == case)
         def _():
-            for copy in rows_out():
+            for copy in rows_out(case):
                 copy.start()
-            own = pltpu.make_async_copy(
-                ybuf.at[e, src : src + count], dobuf.at[e, home : home + count], loc.at[5]
-            )
-            own.start()
-            own.wait()
-            arrive(dobuf.at[f, home : home + count], do_r.at[0])
-            for core in range(2):
-                arrive(dobuf.at[core, mhome : mhome + mcount], do_r.at[1 + core])
-            for copy in rows_out():
-                copy.wait_send()
+
+
+    @pl.when((k == 1))
+    def _():
+        for copy in passed:
+            copy.start()
+
 
     arrive(qbuf.at[f], q_r.at[0])
     for which in range(2):
@@ -215,12 +224,10 @@
     query_col = lax.broadcasted_iota(jnp.int32, (256, 256), 1)
     c2 = SCALE * LOG2E
 
-    def softmax(qb, carry):
+    def scores(qb, carry):
         for head in range(2):
             n = qb * 2 + head
-            cols = slice(128 * head, 128 * head + 128)
-            queries = qbuf[qb, :, cols]
-            dout = dobuf[qb, :, cols]
+            queries = qbuf[qb, :, 128 * head : 128 * head + 128]
             top = jnp.full((1, 256), NEG, F32)
             for jj in range(5):
                 s = dot_nt(kvbuf[0, qb + jj], queries)
@@ -235,21 +242,42 @@
                 )
             top = top * c2
             total = jnp.zeros((1, 256), F32)
-            delta = jnp.zeros((1, 256), F32)
             for jj in range(5):
                 there = 2 * c + qb + jj >= 4
                 p = jnp.exp2(pbuf[n, jj] * c2 - jnp.where(there, top, -NEG))
+                total = total + jnp.sum(p, axis=0, keepdims=True)
+                pbuf[n, jj] = p
+            stats[n, 0:1] = 1.0 / total
+        return carry
+
+    def deltas(qb, carry):
+        for head in range(2):
+            n = qb * 2 + head
+            dout = dobuf[qb, :, 128 * head : 128 * head + 128]
+            delta = jnp.zeros((1, 256), F32)
+            for jj in range(5):
                 dp = dot_nt(kvbuf[1, qb + jj], dout)
-                total = total + jnp.sum(p, axis=0, keepdims=True)
-                delta = delta + jnp.sum(p * dp, axis=0, keepdims=True)
-                pbuf[n, jj] = p
+                delta = delta + jnp.sum(pbuf[n, jj] * dp, axis=0, keepdims=True)
                 dpbuf[n, jj] = dp
-            inverse = 1.0 / total
-            stats[n, 0:1] = inverse
-            stats[n, 1:2] = delta * inverse
+            stats[n, 1:2] = delta * stats[n, 0:1]
         return carry
 
-    lax.fori_loop(0, 2, softmax, 0)
+    lax.fori_loop(0, 2, scores, 0)
+
+    for case in range(ZLO):
+
+        @pl.when(k == case)
+        def _():
+            (src, home, count), (msrc, mhome, mcount), way = ROWS[case]
+            copies = rows_out(case)
+            copies[-1].wait()
+            arrive(dobuf.at[f, home : home + count], do_r.at[0])
+            for core in range(2):
+                arrive(dobuf.at[core, mhome : mhome + mcount], do_r.at[1 + core])
+            for copy in copies[:-1]:
+                copy.wait_send()
+
+    lax.fori_loop(0, 2, deltas, 0)
 
     def terms(j):
         dk = jnp.zeros((256, 128), F32)
@@ -300,7 +328,7 @@
     for d in (1, 2):
         for core in range(2):
             arrive(grecv.at[d - 1, core], gr_r.at[(d - 1) * 2 + core])
-    for copy in sends:
+    for copy in sends + passed:
         copy.wait_send()
 
 

time: 95.2 us -> 92.7 us (0.974)
  the two profiles are of different devices: /device:TPU:7 before, /device:TPU:47 now
where the time goes in v3:
time: 92.7 us; the launch traced here: 92.5 us
  Pallas kernels  91.9 us (99%)
    pallas_call x1, Pallas kernels, on_device(): pl.pallas_call(functools.partial(kernel, chips), out_shape=(jax.ShapeDtyp...  89.5 us
    pallas_call x1, Pallas kernels, on_device(): pl.pallas_call(finish, out_shape=(jax.ShapeDtypeStruct((rows, width), F32...  2.37 us

profile of v3, /device:TPU:47, one launch (start us, length us, event | category | flops | bytes accessed | tf_op | source)
XLA Modules:
  0.0 92.5 jit_solution(8284031185180214614)
XLA Ops:
  0.6 89.5 %band_grads.1 = (f32[256,512]{1,0:T(8,128)}, f32[2,2,256,128]{3,2,1,0:T(8,128)}, bf16[2,2,2,256,128]{4,3,2,1,0:T(8,128)(2,1)}) custom-call(bf16[256,512]{1,0:T(8,128)(2,1)} %q_in.1, bf16[256,256]{1,0:T(8,128)(2,1)} %k_in.1, bf16[256,256]{1,0:T(8,128)(2,1)} %v_in.1, bf16[64,5376]{1,0:T(8,128)(2,1)} %g_in.1, bf16[512,5376]{1,0:T(8,128)(2,1)} %w_in.1), custom_call_target="tpu_custom_call" | custom-call | tf_op jit(solution)/shard_map/band_grads/pallas_call | solution.py:367
  90.2 2.4 %finish.1 = (f32[256,512]{1,0:T(8,128)}, f32[256,256]{1,0:T(8,128)}, f32[256,256]{1,0:T(8,128)}) custom-call(f32[256,512]{1,0:T(8,128)} %get-tuple-element.6.gq_in, f32[2,2,256,128]{3,2,1,0:T(8,128)} %get-tuple-element.7.base_in, bf16[2,2,2,256,128]{4,3,2,1,0:T(8,128)(2,1)} %get-tuple-element.8.grecv_in), custom_call_target="tpu_custom_call" | custom-call | tf_op jit(solution)/shard_map/finish/pallas_call | solution.py:411

commit v4 on v3

--- a/solution.py
+++ b/solution.py
@@ -73,6 +73,26 @@
     def arrive(dst, rs):
         remote(dst, dst, rs, rs, partner).wait_recv()
 
+    barrier = pltpu.get_barrier_semaphore()
+
+    def greet(dev):
+        pl.semaphore_signal(barrier, inc=1, device_id=dev, device_id_type=MESH)
+
+    back = jnp.where(k < 2, 1, -1)
+    greet(partner)
+    greet(plane(1, 1))
+    greet(plane(-1, 1))
+    greet(group(back, 0))
+    for d in (1, 2, -1, -2):
+        greet(chip(d, 0))
+
+    sends = []
+
+    def send(*args):
+        copy = remote(*args)
+        copy.start()
+        sends.append(copy)
+
     def lane(i, n):
         return pl.ds(pl.multiple_of(i * n, n), n)
 
@@ -85,26 +105,6 @@
     ]
     for copy in local:
         copy.start()
-
-    barrier = pltpu.get_barrier_semaphore()
-
-    def greet(dev):
-        pl.semaphore_signal(barrier, inc=1, device_id=dev, device_id_type=MESH)
-
-    back = jnp.where(k < 2, 1, -1)
-    greet(partner)
-    greet(plane(1, 1))
-    greet(plane(-1, 1))
-    greet(group(back, 0))
-    for d in (1, 2, -1, -2):
-        greet(chip(d, 0))
-
-    sends = []
-
-    def send(*args):
-        copy = remote(*args)
-        copy.start()
-        sends.append(copy)
 
     @pl.when(e == 1)
     def _():
@@ -333,26 +333,34 @@
 
 
 def finish(gq_in, base_in, grecv_in, gq_out, gk_out, gv_out, gq, base, grecv, ost, sems):
-    loads = [
-        pltpu.make_async_copy(base_in, base, sems.at[0]),
-        pltpu.make_async_copy(grecv_in, grecv, sems.at[1]),
-        pltpu.make_async_copy(gq_in, gq, sems.at[2]),
-    ]
-    for copy in loads:
-        copy.start()
-    loads[2].wait()
-    outs = [pltpu.make_async_copy(gq, gq_out, sems.at[3])]
-    outs[0].start()
-    loads[0].wait()
-    loads[1].wait()
+    loads = []
+    for which in range(2):
+        loads.append(
+            (
+                pltpu.make_async_copy(base_in.at[:, which], base.at[:, which], sems.at[which]),
+                pltpu.make_async_copy(
+                    grecv_in.at[:, :, which], grecv.at[:, :, which], sems.at[2 + which]
+                ),
+            )
+        )
+    straight = pltpu.make_async_copy(gq_in, gq, sems.at[4])
+    for pair in loads:
+        for copy in pair:
+            copy.start()
+    straight.start()
+    outs = []
     for which, out in ((0, gk_out), (1, gv_out)):
+        for copy in loads[which]:
+            copy.wait()
         for h in range(2):
             ost[which, :, 128 * h : 128 * h + 128] = (
                 base[h, which] + grecv[0, h, which].astype(F32) + grecv[1, h, which].astype(F32)
             )
-        copy = pltpu.make_async_copy(ost.at[which], out, sems.at[4 + which])
-        copy.start()
-        outs.append(copy)
+        outs.append(pltpu.make_async_copy(ost.at[which], out, sems.at[5 + which]))
+        outs[-1].start()
+    straight.wait()
+    outs.append(pltpu.make_async_copy(gq, gq_out, sems.at[7]))
+    outs[-1].start()
     for copy in outs:
         copy.wait()
 
@@ -422,7 +430,7 @@
             vmem((2, 2, 256, 128), F32),
             vmem((2, 2, 2, 256, 128), BF16),
             vmem((2, rows, kv_width), F32),
-            dma((6,)),
+            dma((8,)),
         ],
         name="finish",
     )(gq, base, grecv)

time: 92.7 us -> 92.5 us (level)
  the two profiles are of different devices: /device:TPU:47 before, /device:TPU:59 now
where the time goes in v4:
time: 92.5 us; the launch traced here: 92.4 us
  Pallas kernels  91.8 us (99%)
    pallas_call x1, Pallas kernels, on_device(): pl.pallas_call(functools.partial(kernel, chips), out_shape=(jax.ShapeDtyp...  89.5 us
    pallas_call x1, Pallas kernels, on_device(): pl.pallas_call(finish, out_shape=(jax.ShapeDtypeStruct((rows, width), F32...  2.22 us

profile of v4, /device:TPU:59, one launch (start us, length us, event | category | flops | bytes accessed | tf_op | source)
XLA Modules:
  0.0 92.4 jit_solution(14837718259744839916)
XLA Ops:
  0.6 89.5 %band_grads.1 = (f32[256,512]{1,0:T(8,128)}, f32[2,2,256,128]{3,2,1,0:T(8,128)}, bf16[2,2,2,256,128]{4,3,2,1,0:T(8,128)(2,1)}) custom-call(bf16[256,512]{1,0:T(8,128)(2,1)} %q_in.1, bf16[256,256]{1,0:T(8,128)(2,1)} %k_in.1, bf16[256,256]{1,0:T(8,128)(2,1)} %v_in.1, bf16[64,5376]{1,0:T(8,128)(2,1)} %g_in.1, bf16[512,5376]{1,0:T(8,128)(2,1)} %w_in.1), custom_call_target="tpu_custom_call" | custom-call | tf_op jit(solution)/shard_map/band_grads/pallas_call | solution.py:375
  90.2 2.2 %finish.1 = (f32[256,512]{1,0:T(8,128)}, f32[256,256]{1,0:T(8,128)}, f32[256,256]{1,0:T(8,128)}) custom-call(f32[256,512]{1,0:T(8,128)} %get-tuple-element.6.gq_in, f32[2,2,256,128]{3,2,1,0:T(8,128)} %get-tuple-element.7.base_in, bf16[2,2,2,256,128]{4,3,2,1,0:T(8,128)(2,1)} %get-tuple-element.8.grecv_in), custom_call_target="tpu_custom_call" | custom-call | tf_op jit(solution)/shard_map/finish/pallas_call | solution.py:419
